TPU v7x, 32 devices: a whole 2x2x4 slice. The times are simulated.
32 devices in a mesh: dap: 8 (over y, x, core), dp: 4 (over z).
Axes of the slice: x: 2, y: 2, z: 4, core: 2. Of those that a mesh axis runs over, the one named last changes fastest.
Arguments:
- pair: bfloat16 [64, 16, 128], P(('dp', 'dap')), parts along dimension 0, may hold values from -6 to 6
- pair_mask: int32 [64, 16], P(('dp', 'dap')), parts along dimension 0, may hold values from 0 to 1, as said below
- w_left: bfloat16 [128, 256], replicated, may hold values from -0.5 to 0.5
- w_right: bfloat16 [128, 256], replicated, may hold values from -0.5 to 0.5
- w_tri_gate: bfloat16 [128, 128], replicated, may hold values from -0.5 to 0.5
- w_tri_out: bfloat16 [128, 128], replicated, may hold values from -0.5 to 0.5
- w_attend: bfloat16 [128, 512], replicated, may hold values from -0.5 to 0.5
- w_bias: bfloat16 [128, 4], replicated
- w_att_out: bfloat16 [128, 128], replicated, may hold values from -0.5 to 0.5
Outputs:
- pair_out: float32 [64, 16, 128], P('dp', 'dap'), parts along dimension 0
There are 4 independent parts, one for each index of `dp`. A program takes and returns all parts, laid end to end along the dimension named above; an argument that names none is the same for every part. Nothing has to cross between parts.
Inputs may be any that keep to these rules, and one draw needn't show every extreme that they name: pair_mask[i, i] = 1 for every residue i.
All inputs are finite; a program needn't handle non-finite values.
Results may differ from a plain program's by a relative error of at most 0.014.
The roundings to bfloat16 on the way count: a program that leaves them out, or rounds other values in their place, can miss the bound.
Values may be sent and summed in bfloat16 or wider, within the bound.
No kernel may reach another device: no remote copies, remote signals or barrier semaphores. Data moves between devices by JAX's collectives and lax.ppermute only.
A program may use at most 128 MiB of HBM per device.

v0:
```python
import jax
import jax.numpy as jnp
from jax import lax
from jax.sharding import PartitionSpec as P


def layer_norm(x):
    x = x.astype(jnp.float32)
    mean = jnp.mean(x, axis=-1, keepdims=True)
    var = jnp.mean((x - mean) * (x - mean), axis=-1, keepdims=True)
    return (x - mean) / jnp.sqrt(var + 1e-05)


def matmul(x, w):
    flat = x.reshape(-1, x.shape[-1])
    return jnp.dot(flat, w, preferred_element_type=jnp.float32).reshape(
        x.shape[:-1] + (w.shape[1],)
    )


def edges(zn, weight, maskf, hidden):
    both = matmul(zn, weight)
    return (jax.nn.sigmoid(both[..., :hidden]) * both[..., hidden:] * maskf[..., None]).astype(
        jnp.bfloat16
    )


def triangle_update(pair_part, zn_part, tri, w_tri_gate, w_tri_out):
    tn = layer_norm(tri).astype(jnp.bfloat16)
    update = jax.nn.sigmoid(matmul(zn_part, w_tri_gate)) * matmul(tn, w_tri_out)
    return pair_part.astype(jnp.float32) + update


def attention(pair1, mask_cols, w_attend, w_bias, w_att_out):
    inner = w_att_out.shape[0]
    heads = w_bias.shape[1]
    head_dim = inner // heads
    total, local = (pair1.shape[0], pair1.shape[1])
    yn = layer_norm(pair1).astype(jnp.bfloat16)
    proj = matmul(yn, w_attend)
    query = proj[..., :inner].astype(jnp.bfloat16).reshape(total, local, heads, head_dim)
    keys = proj[..., inner : 2 * inner].astype(jnp.bfloat16).reshape(total, local, heads, head_dim)
    values = (
        proj[..., 2 * inner : 3 * inner].astype(jnp.bfloat16).reshape(total, local, heads, head_dim)
    )
    gate = jax.nn.sigmoid(proj[..., 3 * inner :])
    bias_part = jnp.einsum("kic,ch->hki", yn, w_bias, preferred_element_type=jnp.float32).astype(
        jnp.bfloat16
    )
    bias = lax.all_gather(bias_part, "dap", axis=2, tiled=True)
    scores = jnp.einsum(
        "irhd,krhd->rhki", query, keys, preferred_element_type=jnp.float32
    ) / jnp.sqrt(jnp.float32(head_dim))
    scores = scores + bias.astype(jnp.float32)[None]
    live = jnp.transpose(mask_cols.astype(jnp.float32))[:, None, :, None]
    scores = jnp.where(live > 0.5, scores, jnp.float32(-1000000000.0))
    weights = jax.nn.softmax(scores, axis=2).astype(jnp.bfloat16)
    summed = jnp.einsum(
        "rhki,krhd->irhd", weights, values, preferred_element_type=jnp.float32
    ).reshape(total, local, inner)
    att = (gate * summed).astype(jnp.bfloat16)
    return pair1 + matmul(att, w_att_out)


def shards(pair, pair_mask, w_left, w_right, w_tri_gate, w_tri_out, w_attend, w_bias, w_att_out):
    hidden = w_tri_out.shape[0]
    maskf = pair_mask.astype(jnp.float32)
    zn = layer_norm(pair).astype(jnp.bfloat16)
    left_edge = edges(zn, w_left, maskf, hidden)
    right_edge = edges(zn, w_right, maskf, hidden)
    pair_cols, mask_cols = (
        lax.all_to_all(pair, "dap", split_axis=1, concat_axis=0, tiled=True),
        lax.all_to_all(
            pair_mask.astype(jnp.bfloat16), "dap", split_axis=1, concat_axis=0, tiled=True
        ),
    )
    tri = jnp.einsum(
        "ikc,jkc->ijc",
        lax.all_gather(left_edge, "dap", axis=0, tiled=True),
        right_edge,
        preferred_element_type=jnp.float32,
    )
    zn_cols = layer_norm(pair_cols).astype(jnp.bfloat16)
    pair1 = triangle_update(pair_cols, zn_cols, tri, w_tri_gate, w_tri_out)
    return attention(pair1, mask_cols, w_attend, w_bias, w_att_out)


def solution(mesh):
    placed = (
        P(("dp", "dap"), None, None),
        P(("dp", "dap"), None),
        P(),
        P(),
        P(),
        P(),
        P(),
        P(),
        P(),
    )
    return jax.shard_map(
        shards, mesh=mesh, in_specs=placed, out_specs=P("dp", "dap", None), check_vma=False
    )
```

profile of v0, /device:TPU:0, one launch (start us, length us, event | category | flops | bytes accessed | tf_op | source)
XLA Modules:
  0.0 41.4 jit_solution(9851496634011292177)
XLA Ops:
  0.0 0.0 copy-start
  0.0 0.8 %fusion.56 = (bf16[2,16]{1,0:T(2,128)(2,1)S(1)}, f32[2,16]{1,0:T(2,128)S(1)}) fusion(s32[2,16]{1,0:T(2,128)} %param.10), kind=kLoop, calls=%fused_computation.85 | loop fusion | flops 64 | bytes 320 | tf_op jit(solution)/shard_map/convert_element_type | solution.py:74
  0.8 0.1 all_to_all.8
  0.8 0.0 copy-start.1
  0.8 0.6 %copy.53 = bf16[2,8,2]{2,0,1:T(2,128)(2,1)} copy(bf16[2,8,2]{2,1,0:T(8,128)(2,1)S(1)} %all_to_all.8) | data formatting | bytes 128 | tf_op jit(solution)/shard_map/all_to_all | solution.py:73
  1.5 5.2 %all-to-all-start.1 = ((bf16[2,8,2]{2,0,1:T(2,128)(2,1)}), bf16[2,8,2]{2,0,1:T(2,128)(2,1)S(1)}, u32[]{:S(2)}, u32[]{:S(2)}) async-start(bf16[2,8,2]{2,0,1:T(2,128)(2,1)} %copy.53), calls=%async_computation.1 | async-start | bytes 8192 | tf_op jit(solution)/shard_map/all_to_all | solution.py:73
  6.7 0.0 copy-done.1
  6.7 0.1 convert_reduce_fusion
  6.7 0.2 fusion.25
  6.9 0.0 copy-start.4
  6.9 1.1 %fusion.12 = f32[2,16,256]{2,1,0:T(8,128)S(1)} fusion(bf16[128,256]{1,0:T(8,128)(2,1)} %param.11, bf16[2,16,128]{2,1,0:T(8,128)(2,1)S(1)} %copy-done.1, f32[2,16]{1,0:T(2,128)S(1)} %add_sqrt_fusion.3, f32[2,16]{1,0:T(2,128)S(1)} %broadcast_multiply_fusion.3), kind=kOutput, calls=%fused_computation.18 | convolution fusion | flops 2113536 | bytes 106752 | tf_op jit(solution)/shard_map/dot_general | solution.py:16
  8.0 0.0 copy-done.4
  8.0 0.2 fusion.14
  8.2 0.1 fusion.32
  8.3 9.7 %all_gather.6 = bf16[16,16,128]{2,1,0:T(8,128)(2,1)S(1)} all-gather(bf16[2,16,128]{2,1,0:T(8,128)(2,1)S(1)} %get-tuple-element.10), channel_id=1, replica_groups=mesh['dap'=8,'dp'=4] {'dap'}, dimensions={0}, use_global_device_ids=true | all-gather | bytes 73728 | tf_op jit(solution)/shard_map/all_gather | solution.py:79
  18.0 0.4 %copy.51 = bf16[16,16,128]{1,0,2:T(8,128)(2,1)S(1)} copy(bf16[16,16,128]{2,1,0:T(8,128)(2,1)S(1)} %all_gather.6) | data formatting | bytes 131072 | tf_op jit(solution)/shard_map/all_gather | solution.py:79
  18.4 0.1 copy.50
  18.6 0.4 fusion.60
  18.9 0.1 copy.52
  19.0 0.1 bitcast_reduce_fusion
  19.1 0.2 multiply_reduce_fusion.1
  19.3 0.6 %copy.48 = bf16[2,16,128]{2,0,1:T(2,128)(2,1)} copy(bf16[2,16,128]{2,1,0:T(8,128)(2,1)S(1)} %copy-done.1) | data formatting | bytes 16384 | tf_op args[0]
  19.9 0.0 all-to-all-done.1
  19.9 3.3 %all-to-all-start = ((bf16[2,16,128]{2,0,1:T(2,128)(2,1)}), bf16[2,16,128]{2,0,1:T(2,128)(2,1)S(1)}, u32[]{:S(2)}, u32[]{:S(2)}) async-start(bf16[2,16,128]{2,0,1:T(2,128)(2,1)} %copy.48), calls=%async_computation | async-start | bytes 16384 | tf_op jit(solution)/shard_map/all_to_all | solution.py:72
  23.3 0.1 copy.63
  23.4 4.5 %all-to-all-done = bf16[2,16,128]{2,0,1:T(2,128)(2,1)S(1)} async-done(((bf16[2,16,128]{2,0,1:T(2,128)(2,1)}), bf16[2,16,128]{2,0,1:T(2,128)(2,1)S(1)}, u32[]{:S(2)}, u32[]{:S(2)}) %all-to-all-start) | async-done | bytes 8224 | tf_op jit(solution)/shard_map/all_to_all | solution.py:72
  27.9 0.1 bitcast_reduce_fusion.1
  28.0 0.2 fusion.42
  28.2 0.0 copy-start.5
  28.2 0.1 div.87
  28.3 0.1 sqrt.36
  28.4 0.6 %copy-done.5 = bf16[128,128]{1,0:T(8,128)(2,1)S(1)} copy-done((bf16[128,128]{1,0:T(8,128)(2,1)S(1)}, bf16[128,128]{1,0:T(8,128)(2,1)}, u32[]{:S(2)}) %copy-start.5) | copy-done | bytes 32792
  29.0 0.0 copy-start.6
  29.0 0.2 fusion.8
  29.2 0.6 %copy-done.6 = bf16[128,128]{1,0:T(8,128)(2,1)S(1)} copy-done((bf16[128,128]{1,0:T(8,128)(2,1)S(1)}, bf16[128,128]{1,0:T(8,128)(2,1)}, u32[]{:S(2)}) %copy-start.6) | copy-done | bytes 32792
  29.7 0.3 fusion.57
  30.0 0.2 multiply_reduce_fusion
  30.2 0.1 divide_convert_fusion.2
  30.3 0.0 copy-done
  30.3 0.1 fusion.58
  30.4 0.1 reshape.135
  30.5 0.0 copy-start.3
  30.5 0.1 reshape.136
  30.6 0.6 %copy-done.3 = bf16[128,4]{0,1:T(4,128)(2,1)S(1)} copy-done((bf16[128,4]{0,1:T(4,128)(2,1)S(1)}, bf16[128,4]{0,1:T(4,128)(2,1)}, u32[]{:S(2)}) %copy-start.3) | copy-done | bytes 1048
  31.2 0.1 fusion.9
  31.3 8.0 %all_gather.7 = bf16[4,16,16]{1,0,2:T(4,128)(2,1)S(1)} all-gather(bf16[4,16,2]{1,0,2:T(4,128)(2,1)S(1)} %fusion.9), channel_id=1, replica_groups=mesh['dap'=8,'dp'=4] {'dap'}, dimensions={2}, use_global_device_ids=true | all-gather | bytes 2304 | tf_op jit(solution)/shard_map/all_gather | solution.py:50
  39.3 0.1 copy.57
  39.4 0.1 fusion.4
  39.6 0.1 reshape.134
  39.7 0.2 convolution_bitcast_fusion
  39.9 0.0 copy-start.2
  39.9 0.1 reshape.137
  40.0 0.7 %copy-done.2 = bf16[128,128]{1,0:T(8,128)(2,1)S(1)} copy-done((bf16[128,128]{1,0:T(8,128)(2,1)S(1)}, bf16[128,128]{1,0:T(8,128)(2,1)}, u32[]{:S(2)}) %copy-start.2) | copy-done | bytes 32792
  40.7 0.1 convolution_add_fusion
  40.8 0.6 %copy.61 = f32[16,2,128]{2,1,0:T(2,128)} copy(f32[16,2,128]{2,0,1:T(8,128)S(1)} %convolution_add_fusion) | data formatting | bytes 32768 | tf_op jit(solution)/shard_map/add | solution.py:62
  (16 shorter events, 0.2 us)
Async XLA Ops:
  0.0 30.3 %copy-start = (bf16[128,512]{1,0:T(8,128)(2,1)S(1)}, bf16[128,512]{1,0:T(8,128)(2,1)}, u32[]{:S(2)}) copy-start(bf16[128,512]{1,0:T(8,128)(2,1)} %param.15) | copy-start | bytes 393220
  0.8 5.8 %copy-start.1 = (bf16[2,16,128]{2,1,0:T(8,128)(2,1)S(1)}, bf16[2,16,128]{2,1,0:T(8,128)(2,1)}, u32[]{:S(2)}) copy-start(bf16[2,16,128]{2,1,0:T(8,128)(2,1)} %param.9) | copy-start | bytes 24580
  1.5 18.5 %all-to-all-start.1 = ((bf16[2,8,2]{2,0,1:T(2,128)(2,1)}), bf16[2,8,2]{2,0,1:T(2,128)(2,1)S(1)}, u32[]{:S(2)}, u32[]{:S(2)}) async-start(bf16[2,8,2]{2,0,1:T(2,128)(2,1)} %copy.53), calls=%async_computation.1 | async-start | bytes 8192 | tf_op jit(solution)/shard_map/all_to_all | solution.py:73
  6.9 1.1 %copy-start.4 = (bf16[128,256]{1,0:T(8,128)(2,1)S(1)}, bf16[128,256]{1,0:T(8,128)(2,1)}, u32[]{:S(2)}) copy-start(bf16[128,256]{1,0:T(8,128)(2,1)} %param.12) | copy-start | bytes 196612
  19.9 8.0 %all-to-all-start = ((bf16[2,16,128]{2,0,1:T(2,128)(2,1)}), bf16[2,16,128]{2,0,1:T(2,128)(2,1)S(1)}, u32[]{:S(2)}, u32[]{:S(2)}) async-start(bf16[2,16,128]{2,0,1:T(2,128)(2,1)} %copy.48), calls=%async_computation | async-start | bytes 16384 | tf_op jit(solution)/shard_map/all_to_all | solution.py:72
  28.2 0.8 %copy-start.5 = (bf16[128,128]{1,0:T(8,128)(2,1)S(1)}, bf16[128,128]{1,0:T(8,128)(2,1)}, u32[]{:S(2)}) copy-start(bf16[128,128]{1,0:T(8,128)(2,1)} %param.13) | copy-start | bytes 98308
  29.0 0.8 %copy-start.6 = (bf16[128,128]{1,0:T(8,128)(2,1)S(1)}, bf16[128,128]{1,0:T(8,128)(2,1)}, u32[]{:S(2)}) copy-start(bf16[128,128]{1,0:T(8,128)(2,1)} %param.14) | copy-start | bytes 98308
  30.5 0.7 %copy-start.3 = (bf16[128,4]{0,1:T(4,128)(2,1)S(1)}, bf16[128,4]{0,1:T(4,128)(2,1)}, u32[]{:S(2)}) copy-start(bf16[128,4]{0,1:T(4,128)(2,1)} %param.16) | copy-start | bytes 3076
  39.9 0.8 %copy-start.2 = (bf16[128,128]{1,0:T(8,128)(2,1)S(1)}, bf16[128,128]{1,0:T(8,128)(2,1)}, u32[]{:S(2)}) copy-start(bf16[128,128]{1,0:T(8,128)(2,1)} %param.17) | copy-start | bytes 98308
where the time goes:
time: 42 us; the launch traced here: 41.4 us
  blocking collectives  17.7 us (42%)
  starting transfers between devices  8.53 us (20%)
  local copies, waits for them, and re-layouts  5.7 us (14%)
  waiting for transfers between devices  4.51 us (11%)
  matrix products  2.83 us (7%)
  other arithmetic  1.97 us (5%)
    all_gather x1, blocking collectives, shards(): lax.all_gather(left_edge, 'dap', axis=0, tiled=True)  9.75 us
    all_gather x1, blocking collectives, attention(): bias = lax.all_gather(bias_part, 'dap', axis=2, tiled=True)  7.98 us
    all_to_all x1, starting transfers between devices, shards(): lax.all_to_all(pair_mask.astype(jnp.bfloat16), 'dap', split_axis=1, conca...  5.2 us
    all_to_all x1, waiting for transfers between devices, shards(): lax.all_to_all(pair, 'dap', split_axis=1, concat_axis=0, tiled=True)  4.51 us
    all_to_all x1, starting transfers between devices, shards(): lax.all_to_all(pair, 'dap', split_axis=1, concat_axis=0, tiled=True)  3.33 us
    unnamed x15, local copies, waits for them, and re-layouts  3 us
    dot_general x6, matrix products, matmul(): jnp.dot(flat, w, preferred_element_type=jnp.float32)  1.99 us
  transfers between devices with their start and end apart: 2, of which 1 were waited for; matrix products, arithmetic and copies ran while one was open for 9% of the time, Pallas kernels for 0%

commit v1 on v0

--- a/solution.py
+++ b/solution.py
@@ -2,6 +2,14 @@
 import jax.numpy as jnp
 from jax import lax
 from jax.sharding import PartitionSpec as P
+
+
+def reach_the_series_all(field, in_dim):
+    field = jnp.moveaxis(field, 0, in_dim)
+    field_out = field.shape
+    return field.reshape(
+        *field_out[:in_dim], field_out[in_dim] * field_out[in_dim + 1], *field_out[in_dim + 2 :]
+    )
 
 
 def layer_norm(x):
@@ -74,12 +82,23 @@
             pair_mask.astype(jnp.bfloat16), "dap", split_axis=1, concat_axis=0, tiled=True
         ),
     )
-    tri = jnp.einsum(
-        "ikc,jkc->ijc",
-        lax.all_gather(left_edge, "dap", axis=0, tiled=True),
-        right_edge,
-        preferred_element_type=jnp.float32,
-    )
+    w_next = lax.axis_size("dap")
+    s_next = lax.axis_index("dap")
+    formed, then, e_now = (w_next, s_next, left_edge.shape[0])
+    all_blocks = []
+    for pp in [*range(formed)]:
+        all_blocks.append((pp, (pp + 1) % formed))
+    entries = []
+    b_now = left_edge
+    for ii in [*range(formed)]:
+        vec_out = b_now if ii == formed - 1 else lax.ppermute(b_now, "dap", all_blocks)
+        state_now = jnp.einsum(
+            "ikc,jkc->ijc", b_now, right_edge, preferred_element_type=jnp.float32
+        )
+        entries.append(state_now)
+        b_now = vec_out
+    entries = jnp.stack(entries)[(then - jnp.arange(formed)) % formed]
+    tri = reach_the_series_all(entries, 0)
     zn_cols = layer_norm(pair_cols).astype(jnp.bfloat16)
     pair1 = triangle_update(pair_cols, zn_cols, tri, w_tri_gate, w_tri_out)
     return attention(pair1, mask_cols, w_attend, w_bias, w_att_out)

time: 42 us -> 62.9 us (1.50)
  waiting for transfers between devices: 4.51 us -> 29.7 us
  blocking collectives: 17.7 us -> 7.97 us
  local copies, waits for them, and re-layouts: 5.7 us -> 8.08 us
  matrix products: 2.83 us -> 5.09 us
  starting transfers between devices: 8.53 us -> 9.17 us
    ppermute x0 -> x7, waiting for transfers between devices: none -> 21.7 us  [shards(): lax.ppermute(b_now, 'dap', all_blocks)]
    all_gather x1 -> x0, blocking collectives: 9.75 us -> none  [shards(): lax.all_gather(left_edge, 'dap', axis=0, tiled=True)]
    all_to_all x1, waiting for transfers between devices: 0.01 us -> 3.5 us  [shards(): lax.all_to_all(pair_mask.astype(jnp.bfloat16), 'dap', split_axis=1, conca...]
    dot_general x1 -> x8, matrix products: 0.37 us -> 2.63 us  [shards(): jnp.einsum('ikc,jkc->ijc', b_now, right_edge, preferred_element_type=jnp....]
    ppermute x0 -> x7, local copies, waits for them, and re-layouts: none -> 0.88 us  [shards(): lax.ppermute(b_now, 'dap', all_blocks)]
    ppermute x0 -> x7, starting transfers between devices: none -> 0.85 us  [shards(): lax.ppermute(b_now, 'dap', all_blocks)]
    reduce_sum x3, other arithmetic: 0.26 us -> 1.03 us  [layer_norm(): mean = jnp.mean(x, axis=-1, keepdims=True)]
    convert_element_type x1, other arithmetic: 0.76 us -> 0.01 us  [shards(): pair_mask.astype(jnp.bfloat16)]
  transfers between devices with their start and end apart: 2 -> 9, of which waited for: 1 -> 8; matrix products, arithmetic and copies ran while one was open for 9% -> 7% of each run, Pallas kernels for 0% -> 0%
where the time goes in v1:
time: 62.9 us; the launch traced here: 62.4 us
  waiting for transfers between devices  29.7 us (47%)
  starting transfers between devices  9.17 us (15%)
  local copies, waits for them, and re-layouts  8.08 us (13%)
  blocking collectives  7.97 us (13%)
  matrix products  5.09 us (8%)
  other arithmetic  2 us (3%)
    ppermute x7, waiting for transfers between devices, shards(): lax.ppermute(b_now, 'dap', all_blocks)  21.7 us
    all_gather x1, blocking collectives, attention(): bias = lax.all_gather(bias_part, 'dap', axis=2, tiled=True)  7.97 us
    all_to_all x1, starting transfers between devices, shards(): lax.all_to_all(pair_mask.astype(jnp.bfloat16), 'dap', split_axis=1, conca...  4.99 us
    all_to_all x1, waiting for transfers between devices, shards(): lax.all_to_all(pair, 'dap', split_axis=1, concat_axis=0, tiled=True)  4.51 us
    all_to_all x1, waiting for transfers between devices, shards(): lax.all_to_all(pair_mask.astype(jnp.bfloat16), 'dap', split_axis=1, conca...  3.5 us
    unnamed x17, local copies, waits for them, and re-layouts  3.34 us
    all_to_all x1, starting transfers between devices, shards(): lax.all_to_all(pair, 'dap', split_axis=1, concat_axis=0, tiled=True)  3.33 us
    dot_general x8, matrix products, shards(): jnp.einsum('ikc,jkc->ijc', b_now, right_edge, preferred_element_type=jnp....  2.63 us
  transfers between devices with their start and end apart: 9, of which 8 were waited for; matrix products, arithmetic and copies ran while one was open for 7% of the time, Pallas kernels for 0%

profile of v1, /device:TPU:0, one launch (start us, length us, event | category | flops | bytes accessed | tf_op | source)
XLA Modules:
  0.0 62.4 jit_solution(12825366767834870501)
XLA Ops:
  0.0 0.9 %convert_reduce_fusion = f32[2,16]{1,0:T(2,128)S(1)} fusion(bf16[2,16,128]{2,1,0:T(8,128)(2,1)} %param.9), kind=kLoop, calls=%fused_computation.48 | loop fusion | flops 8160 | bytes 8320 | tf_op jit(solution)/shard_map/reduce_sum | solution.py:17
  0.9 0.2 fusion.33
  1.0 1.1 %fusion.20 = f32[2,16,256]{2,1,0:T(8,128)S(1)} fusion(bf16[128,256]{1,0:T(8,128)(2,1)} %param.11, bf16[2,16,128]{2,1,0:T(8,128)(2,1)S(1)} %copy-done.1, f32[2,16]{1,0:T(2,128)S(1)} %add_sqrt_fusion.3, f32[2,16]{1,0:T(2,128)S(1)} %broadcast_multiply_fusion.3), kind=kOutput, calls=%fused_computation.35 | convolution fusion | flops 2113536 | bytes 106752 | tf_op jit(solution)/shard_map/dot_general | solution.py:24
  2.1 0.2 fusion.22
  2.3 0.5 copy-done.3
  2.9 0.5 collective-permute-start
  3.4 0.1 all_to_all.8
  3.5 0.6 copy.254
  4.1 5.0 %all-to-all-start.1 = ((bf16[2,8,2]{2,0,1:T(2,128)(2,1)}), bf16[2,8,2]{2,0,1:T(2,128)(2,1)S(1)}, u32[]{:S(2)}, u32[]{:S(2)}) async-start(bf16[2,8,2]{2,0,1:T(2,128)(2,1)} %copy.254), calls=%async_computation.1 | async-start | bytes 8192 | tf_op jit(solution)/shard_map/all_to_all | solution.py:81
  9.1 0.1 copy.231
  9.2 0.1 copy.230
  9.3 0.3 fusion.8
  9.6 0.6 copy.228
  10.2 3.5 %all-to-all-done.1 = bf16[2,8,2]{2,0,1:T(2,128)(2,1)S(1)} async-done(((bf16[2,8,2]{2,0,1:T(2,128)(2,1)}), bf16[2,8,2]{2,0,1:T(2,128)(2,1)S(1)}, u32[]{:S(2)}, u32[]{:S(2)}) %all-to-all-start.1) | async-done | bytes 96 | tf_op jit(solution)/shard_map/all_to_all | solution.py:81
  13.7 3.3 %all-to-all-start = ((bf16[2,16,128]{2,0,1:T(2,128)(2,1)}), bf16[2,16,128]{2,0,1:T(2,128)(2,1)S(1)}, u32[]{:S(2)}, u32[]{:S(2)}) async-start(bf16[2,16,128]{2,0,1:T(2,128)(2,1)} %copy.228), calls=%async_computation | async-start | bytes 16384 | tf_op jit(solution)/shard_map/all_to_all | solution.py:80
  17.1 0.1 copy.264
  17.2 4.5 %all-to-all-done = bf16[2,16,128]{2,0,1:T(2,128)(2,1)S(1)} async-done(((bf16[2,16,128]{2,0,1:T(2,128)(2,1)}), bf16[2,16,128]{2,0,1:T(2,128)(2,1)S(1)}, u32[]{:S(2)}, u32[]{:S(2)}) %all-to-all-start) | async-done | bytes 8224 | tf_op jit(solution)/shard_map/all_to_all | solution.py:80
  21.7 0.1 bitcast_reduce_fusion
  21.8 0.2 fusion.50
  22.2 0.6 copy-done.6
  22.8 0.2 fusion.16
  23.0 0.1 copy.233
  23.2 0.3 fusion.7
  23.5 3.6 %collective-permute-done.1 = bf16[2,16,128]{2,1,0:T(8,128)(2,1)S(1)} collective-permute-done((bf16[2,16,128]{2,1,0:T(8,128)(2,1)S(1)}, bf16[2,16,128]{2,1,0:T(8,128)(2,1)S(1)}, u32[]{:S(2)}, u32[]{:S(2)}) %collective-permute-start.1) | collective-permute-done | bytes 8224 | tf_op jit(solution)/shard_map/ppermute | solution.py:94
  27.1 0.1 copy.235
  27.3 0.3 fusion.6
  27.7 3.6 %collective-permute-done.2 = bf16[2,16,128]{2,1,0:T(8,128)(2,1)S(1)} collective-permute-done((bf16[2,16,128]{2,1,0:T(8,128)(2,1)S(1)}, bf16[2,16,128]{2,1,0:T(8,128)(2,1)S(1)}, u32[]{:S(2)}, u32[]{:S(2)}) %collective-permute-start.2) | collective-permute-done | bytes 8224 | tf_op jit(solution)/shard_map/ppermute | solution.py:94
  31.3 0.1 copy.237
  31.5 0.3 fusion.5
  31.8 3.6 %collective-permute-done.3 = bf16[2,16,128]{2,1,0:T(8,128)(2,1)S(1)} collective-permute-done((bf16[2,16,128]{2,1,0:T(8,128)(2,1)S(1)}, bf16[2,16,128]{2,1,0:T(8,128)(2,1)S(1)}, u32[]{:S(2)}, u32[]{:S(2)}) %collective-permute-start.3) | collective-permute-done | bytes 8224 | tf_op jit(solution)/shard_map/ppermute | solution.py:94
  35.4 0.1 copy.239
  35.6 0.3 fusion.4
  36.0 3.6 %collective-permute-done.4 = bf16[2,16,128]{2,1,0:T(8,128)(2,1)S(1)} collective-permute-done((bf16[2,16,128]{2,1,0:T(8,128)(2,1)S(1)}, bf16[2,16,128]{2,1,0:T(8,128)(2,1)S(1)}, u32[]{:S(2)}, u32[]{:S(2)}) %collective-permute-start.4) | collective-permute-done | bytes 8224 | tf_op jit(solution)/shard_map/ppermute | solution.py:94
  39.6 0.1 copy.241
  39.8 0.3 fusion.3
  40.1 3.6 %collective-permute-done.5 = bf16[2,16,128]{2,1,0:T(8,128)(2,1)S(1)} collective-permute-done((bf16[2,16,128]{2,1,0:T(8,128)(2,1)S(1)}, bf16[2,16,128]{2,1,0:T(8,128)(2,1)S(1)}, u32[]{:S(2)}, u32[]{:S(2)}) %collective-permute-start.5) | collective-permute-done | bytes 8224 | tf_op jit(solution)/shard_map/ppermute | solution.py:94
  43.8 0.1 copy.243
  43.9 0.3 fusion.2
  44.3 3.6 %collective-permute-done.6 = bf16[2,16,128]{2,1,0:T(8,128)(2,1)S(1)} collective-permute-done((bf16[2,16,128]{2,1,0:T(8,128)(2,1)S(1)}, bf16[2,16,128]{2,1,0:T(8,128)(2,1)S(1)}, u32[]{:S(2)}, u32[]{:S(2)}) %collective-permute-start.6) | collective-permute-done | bytes 8224 | tf_op jit(solution)/shard_map/ppermute | solution.py:94
  47.9 0.1 copy.245
  48.0 0.3 fusion.1
  48.4 0.5 copy.246
  48.8 0.6 gather_fusion
  49.4 0.1 reduce_sum.85
  49.5 0.1 copy.249
  49.7 0.1 copy.250
  49.9 0.2 fusion.52
  50.0 0.1 copy.253
  50.2 0.4 copy-done.7
  50.6 0.3 fusion.69
  50.9 0.2 multiply_reduce_fusion
  51.1 0.1 divide_convert_fusion.2
  51.2 0.1 fusion.70
  51.3 0.1 reshape.220
  51.5 0.6 copy-done.4
  52.1 0.1 fusion.17
  52.2 8.0 %all_gather.3 = bf16[4,16,16]{1,0,2:T(4,128)(2,1)S(1)} all-gather(bf16[4,16,2]{1,0,2:T(4,128)(2,1)S(1)} %fusion.17), channel_id=1, replica_groups=mesh['dap'=8,'dp'=4] {'dap'}, dimensions={2}, use_global_device_ids=true | all-gather | bytes 2304 | tf_op jit(solution)/shard_map/all_gather | solution.py:58
  60.2 0.1 copy.258
  60.3 0.1 fusion.12
  60.6 0.2 convolution_bitcast_fusion.8
  60.9 0.1 reshape.222
  60.9 0.7 %copy-done.2 = bf16[128,128]{1,0:T(8,128)(2,1)S(1)} copy-done((bf16[128,128]{1,0:T(8,128)(2,1)S(1)}, bf16[128,128]{1,0:T(8,128)(2,1)}, u32[]{:S(2)}) %copy-start.2) | copy-done | bytes 32792
  61.6 0.1 convolution_add_fusion
  61.7 0.6 copy.262
  (45 shorter events, 1.2 us)
Async XLA Ops:
  0.0 51.2 %copy-start = (bf16[128,512]{1,0:T(8,128)(2,1)S(1)}, bf16[128,512]{1,0:T(8,128)(2,1)}, u32[]{:S(2)}) copy-start(bf16[128,512]{1,0:T(8,128)(2,1)} %param.15) | copy-start | bytes 393220
  0.0 0.9 %copy-start.1 = (bf16[2,16,128]{2,1,0:T(8,128)(2,1)S(1)}, bf16[2,16,128]{2,1,0:T(8,128)(2,1)}, u32[]{:S(2)}) copy-start(bf16[2,16,128]{2,1,0:T(8,128)(2,1)} %param.9) | copy-start | bytes 24580
  1.0 1.1 %copy-start.5 = (bf16[128,256]{1,0:T(8,128)(2,1)S(1)}, bf16[128,256]{1,0:T(8,128)(2,1)}, u32[]{:S(2)}) copy-start(bf16[128,256]{1,0:T(8,128)(2,1)} %param.12) | copy-start | bytes 196612
  2.1 0.7 %copy-start.3 = (s32[2,16]{1,0:T(2,128)S(1)}, s32[2,16]{1,0:T(2,128)}, u32[]{:S(2)}) copy-start(s32[2,16]{1,0:T(2,128)} %param.10) | copy-start | bytes 388
  2.9 20.1 %collective-permute-start = (bf16[2,16,128]{2,1,0:T(8,128)(2,1)S(1)}, bf16[2,16,128]{2,1,0:T(8,128)(2,1)S(1)}, u32[]{:S(2)}, u32[]{:S(2)}) collective-permute-start(bf16[2,16,128]{2,1,0:T(8,128)(2,1)S(1)} %get-tuple-element.10), channel_id=1, source_target_pairs={{0,4},{4,8},{8,12},{12,16},{16,20},{20,24},{24,28},{28,0},{1,5},{5... | collective-permute-start | bytes 24584 | tf_op jit(solution)/shard_map/ppermute | solution.py:94
  4.1 9.7 %all-to-all-start.1 = ((bf16[2,8,2]{2,0,1:T(2,128)(2,1)}), bf16[2,8,2]{2,0,1:T(2,128)(2,1)S(1)}, u32[]{:S(2)}, u32[]{:S(2)}) async-start(bf16[2,8,2]{2,0,1:T(2,128)(2,1)} %copy.254), calls=%async_computation.1 | async-start | bytes 8192 | tf_op jit(solution)/shard_map/all_to_all | solution.py:81
  13.7 8.0 %all-to-all-start = ((bf16[2,16,128]{2,0,1:T(2,128)(2,1)}), bf16[2,16,128]{2,0,1:T(2,128)(2,1)S(1)}, u32[]{:S(2)}, u32[]{:S(2)}) async-start(bf16[2,16,128]{2,0,1:T(2,128)(2,1)} %copy.228), calls=%async_computation | async-start | bytes 16384 | tf_op jit(solution)/shard_map/all_to_all | solution.py:80
  22.0 0.8 %copy-start.6 = (bf16[128,128]{1,0:T(8,128)(2,1)S(1)}, bf16[128,128]{1,0:T(8,128)(2,1)}, u32[]{:S(2)}) copy-start(bf16[128,128]{1,0:T(8,128)(2,1)} %param.13) | copy-start | bytes 98308
  23.1 4.0 %collective-permute-start.1 = (bf16[2,16,128]{2,1,0:T(8,128)(2,1)S(1)}, bf16[2,16,128]{2,1,0:T(8,128)(2,1)S(1)}, u32[]{:S(2)}, u32[]{:S(2)}) collective-permute-start(bf16[2,16,128]{2,1,0:T(8,128)(2,1)S(1)} %collective-permute-done), channel_id=1, source_target_pairs={{0,4},{4,8},{8,12},{12,16},{16,20},{20,24},{24,28},{28,0},{1,5},{5... | collective-permute-start | bytes 24584 | tf_op jit(solution)/shard_map/ppermute | solution.py:94
  27.3 4.0 %collective-permute-start.2 = (bf16[2,16,128]{2,1,0:T(8,128)(2,1)S(1)}, bf16[2,16,128]{2,1,0:T(8,128)(2,1)S(1)}, u32[]{:S(2)}, u32[]{:S(2)}) collective-permute-start(bf16[2,16,128]{2,1,0:T(8,128)(2,1)S(1)} %collective-permute-done.1), channel_id=1, source_target_pairs={{0,4},{4,8},{8,12},{12,16},{16,20},{20,24},{24,28},{28,0},{1,5},{5... | collective-permute-start | bytes 24584 | tf_op jit(solution)/shard_map/ppermute | solution.py:94
  31.4 4.0 %collective-permute-start.3 = (bf16[2,16,128]{2,1,0:T(8,128)(2,1)S(1)}, bf16[2,16,128]{2,1,0:T(8,128)(2,1)S(1)}, u32[]{:S(2)}, u32[]{:S(2)}) collective-permute-start(bf16[2,16,128]{2,1,0:T(8,128)(2,1)S(1)} %collective-permute-done.2), channel_id=1, source_target_pairs={{0,4},{4,8},{8,12},{12,16},{16,20},{20,24},{24,28},{28,0},{1,5},{5... | collective-permute-start | bytes 24584 | tf_op jit(solution)/shard_map/ppermute | solution.py:94
  35.6 4.0 %collective-permute-start.4 = (bf16[2,16,128]{2,1,0:T(8,128)(2,1)S(1)}, bf16[2,16,128]{2,1,0:T(8,128)(2,1)S(1)}, u32[]{:S(2)}, u32[]{:S(2)}) collective-permute-start(bf16[2,16,128]{2,1,0:T(8,128)(2,1)S(1)} %collective-permute-done.3), channel_id=1, source_target_pairs={{0,4},{4,8},{8,12},{12,16},{16,20},{20,24},{24,28},{28,0},{1,5},{5... | collective-permute-start | bytes 24584 | tf_op jit(solution)/shard_map/ppermute | solution.py:94
  39.7 4.0 %collective-permute-start.5 = (bf16[2,16,128]{2,1,0:T(8,128)(2,1)S(1)}, bf16[2,16,128]{2,1,0:T(8,128)(2,1)S(1)}, u32[]{:S(2)}, u32[]{:S(2)}) collective-permute-start(bf16[2,16,128]{2,1,0:T(8,128)(2,1)S(1)} %collective-permute-done.4), channel_id=1, source_target_pairs={{0,4},{4,8},{8,12},{12,16},{16,20},{20,24},{24,28},{28,0},{1,5},{5... | collective-permute-start | bytes 24584 | tf_op jit(solution)/shard_map/ppermute | solution.py:94
  43.9 4.0 %collective-permute-start.6 = (bf16[2,16,128]{2,1,0:T(8,128)(2,1)S(1)}, bf16[2,16,128]{2,1,0:T(8,128)(2,1)S(1)}, u32[]{:S(2)}, u32[]{:S(2)}) collective-permute-start(bf16[2,16,128]{2,1,0:T(8,128)(2,1)S(1)} %collective-permute-done.5), channel_id=1, source_target_pairs={{0,4},{4,8},{8,12},{12,16},{16,20},{20,24},{24,28},{28,0},{1,5},{5... | collective-permute-start | bytes 24584 | tf_op jit(solution)/shard_map/ppermute | solution.py:94
  49.9 0.8 %copy-start.7 = (bf16[128,128]{1,0:T(8,128)(2,1)S(1)}, bf16[128,128]{1,0:T(8,128)(2,1)}, u32[]{:S(2)}) copy-start(bf16[128,128]{1,0:T(8,128)(2,1)} %param.14) | copy-start | bytes 98308
  51.4 0.7 %copy-start.4 = (bf16[128,4]{0,1:T(4,128)(2,1)S(1)}, bf16[128,4]{0,1:T(4,128)(2,1)}, u32[]{:S(2)}) copy-start(bf16[128,4]{0,1:T(4,128)(2,1)} %param.16) | copy-start | bytes 3076
  60.8 0.8 %copy-start.2 = (bf16[128,128]{1,0:T(8,128)(2,1)S(1)}, bf16[128,128]{1,0:T(8,128)(2,1)}, u32[]{:S(2)}) copy-start(bf16[128,128]{1,0:T(8,128)(2,1)} %param.17) | copy-start | bytes 98308
